TPU v7x, 128 devices: a whole 4x4x4 slice. The times are simulated.
128 devices in a mesh: dp: 8 (over y_hi, z), ctx: 16 (over y_lo, x, core).
Axes of the slice: x: 4, y: 4 (y_hi: 2, y_lo: 2; y = y_hi * 2 + y_lo), z: 4, core: 2. Of those that a mesh axis runs over, the one named last changes fastest.
Arguments:
- hidden: bfloat16 [8, 4096, 8192], P('dp', 'ctx'), may hold values from -6 to 6
- queries: bfloat16 [8, 4096, 4096], P('dp', 'ctx')
- layout: int32 [8, 32], P('dp'), may hold values from 0 to 31, each once within a row
- boundary: int32 [8], P('dp'), may hold values from 1 to 4095
- key_matrix: bfloat16 [8192, 512], P(('dp', 'ctx')), may hold values from -0.0625 to 0.0625
- value_matrix: bfloat16 [8192, 512], P(('dp', 'ctx')), may hold values from -0.0625 to 0.0625
Outputs:
- attended: bfloat16 [8, 4096, 4096], P('dp', 'ctx')
Inputs may be any that keep to these rules, and one draw needn't show every extreme that they name: Each row holds every block number of 0 to 31 once; local block b of ctx index c is layout[2 c + b].
All inputs are finite; a program needn't handle non-finite values.
Results may differ from a plain program's by a relative error of at most 0.011.
Values may be sent and summed in bfloat16 or wider, within the bound.
A program may use at most 320 MiB of HBM per device.

v0:
```python
import jax
import jax.numpy as jnp
from jax import lax
from jax.sharding import PartitionSpec as P

HEAD_WIDTH = 128


def shifted(shard, axis, by):
    size = lax.axis_size(axis)
    return lax.ppermute(shard, axis, [(i, (i + by) % size) for i in range(size)])


def per_device(hidden, queries, layout, boundary, key_matrix, value_matrix):
    rows = hidden.shape[1]
    kv_width = key_matrix.shape[1]
    head_size = HEAD_WIDTH
    kv_heads = kv_width // head_size
    group_size = queries.shape[2] // kv_width
    half = rows // 2
    scale = head_size ** (-0.5)
    ctx_count = lax.axis_size("ctx")
    here = lax.axis_index("ctx")
    tokens = hidden[0]
    order = layout[0]
    start_doc = boundary[0]
    block_ids = jnp.arange(order.shape[0], dtype=jnp.int32)

    def positions(first, count):
        index = first + jnp.arange(count, dtype=jnp.int32)
        match = (index // half)[:, None] == block_ids[None, :]
        looked = jnp.sum(jnp.where(match, order[None, :], 0), axis=1)
        return looked * half + index % half

    keys_full = jnp.dot(
        tokens,
        lax.all_gather(key_matrix, ("dp", "ctx"), axis=0, tiled=True),
        preferred_element_type=jnp.float32,
    )
    values_full = jnp.dot(
        tokens,
        lax.all_gather(value_matrix, ("dp", "ctx"), axis=0, tiled=True),
        preferred_element_type=jnp.float32,
    )
    stacked = jnp.stack((keys_full.astype(jnp.bfloat16), values_full.astype(jnp.bfloat16)), axis=0)
    query_rows = queries[0].reshape(rows, kv_heads, group_size, head_size)
    query_pos = positions(here * rows, rows)

    def attend(state, block_list, first):
        count = block_list.shape[1]
        key_pos = positions(first, count)
        allowed = (key_pos[None, :] <= query_pos[:, None]) & (
            (key_pos[None, :] >= start_doc) | (query_pos[:, None] < start_doc)
        )
        running, total, summed = state
        key_row_set = block_list[0].reshape(count, kv_heads, head_size)
        value_row_set = block_list[1].reshape(count, kv_heads, head_size)
        scores = (
            jnp.einsum(
                "qgha,kga->ghqk", query_rows, key_row_set, preferred_element_type=jnp.float32
            )
            * scale
        )
        scores = jnp.where(allowed, scores, -1e30)
        peak = jnp.maximum(running, jnp.max(scores, axis=-1))
        factor = jnp.exp(running - peak)
        weights = jnp.where(allowed, jnp.exp(scores - peak[..., None]), 0.0)
        total = total * factor + jnp.sum(weights, axis=-1)
        probs = weights.astype(jnp.bfloat16)
        summed = summed * factor[..., None] + jnp.einsum(
            "ghqk,kga->ghqa", probs, value_row_set, preferred_element_type=jnp.float32
        )
        return (peak, total, summed)

    initial = (
        jnp.full((kv_heads, group_size, rows), -1e30, jnp.float32),
        jnp.zeros((kv_heads, group_size, rows), jnp.float32),
        jnp.zeros((kv_heads, group_size, rows, head_size), jnp.float32),
    )
    state = attend(initial, stacked, here * rows)

    def turn(step, carry):
        state_now, block_list = carry
        block_list = shifted(block_list, "ctx", 1)
        source = (here - step - 1) % ctx_count
        return (attend(state_now, block_list, source * rows), block_list)

    state, unused_blocks = lax.fori_loop(0, ctx_count - 1, turn, (state, stacked))
    running, total, summed = state
    result = summed / total[..., None]
    result = result.transpose(2, 0, 1, 3).reshape(rows, kv_heads * group_size * head_size)
    return result.astype(jnp.bfloat16)[None]


def solution(mesh):
    in_specs = (
        P("dp", "ctx", None),
        P("dp", "ctx", None),
        P("dp", None),
        P("dp"),
        P(("dp", "ctx"), None),
        P(("dp", "ctx"), None),
    )
    out_specs = P("dp", "ctx", None)
    return jax.shard_map(
        per_device, mesh=mesh, in_specs=in_specs, out_specs=out_specs, check_vma=False
    )
```

profile of v0, /device:TPU:0, one launch (start us, length us, event | category | flops | bytes accessed | tf_op | source)
XLA Modules:
  0.0 751.3 jit_solution(1733711466814543764)
XLA Ops:
  8.7 4.1 copy.26
  16.1 198.8 %all-gather.5.cloned.1.call-done = bf16[8192,512]{1,0:T(8,128)(2,1)} async-done(((bf16[64,512]{1,0:T(8,128)(2,1)}), bf16[8192,512]{1,0:T(8,128)(2,1)}) %all-gather.5.cloned.1.call-update) | async-done | bytes 8388624 | tf_op jit(solution)/shard_map/all_gather | solution.py:42
  214.9 7.0 fusion.39
  222.6 195.6 %all-gather.3.cloned.1.call-done = bf16[8192,512]{1,0:T(8,128)(2,1)} async-done(((bf16[64,512]{1,0:T(8,128)(2,1)}), bf16[8192,512]{1,0:T(8,128)(2,1)}) %all-gather.3.cloned.1.call-update) | async-done | bytes 8388624 | tf_op jit(solution)/shard_map/all_gather | solution.py:37
  418.2 7.0 fusion.36
  431.0 4.7 broadcast_add_fusion
  435.7 302.3 %while.23 = (s32[]{:T(128)}, f32[4,8,256]{2,1,0:T(8,128)S(1)}, f32[4,8,256]{2,1,0:T(8,128)S(1)}, f32[4,8,256,128]{3,2,1,0:T(8,128)}, bf16[2,256,512]{1,2,0:T(8,1...) while((s32[]{:T(128)}, f32[4,8,256]{2,1,0:T(8,128)S(1)}, ...), condition=%wide.region_7.8_spmd.clone, body=%wide.region_3.7_spmd.clone.sunk | while | flops 1103347456 | bytes 74720784 | solution.py:88
  436.6 9.8 %collective-permute-done = bf16[2,256,512]{1,2,0:T(8,128)(2,1)S(1)} collective-permute-done((bf16[2,256,512]{1,2,0:T(8,128)(2,1)S(1)}, bf16[2,256,512]{1,2,0:T(8,128)(2,1)S(1)}, u32[]{:S(2)}, u32[]{:S(2)}) %collective-permute-start) | collective-permute-done | bytes 524320 | tf_op jit(solution)/shard_map/while/body/eval_jaxpr/ppermute | solution.py:11
  450.2 3.7 multiply_add_fusion.5
  456.8 9.8 %collective-permute-done = bf16[2,256,512]{1,2,0:T(8,128)(2,1)S(1)} collective-permute-done((bf16[2,256,512]{1,2,0:T(8,128)(2,1)S(1)}, bf16[2,256,512]{1,2,0:T(8,128)(2,1)S(1)}, u32[]{:S(2)}, u32[]{:S(2)}) %collective-permute-start) | collective-permute-done | bytes 524320 | tf_op jit(solution)/shard_map/while/body/eval_jaxpr/ppermute | solution.py:11
  470.3 3.7 multiply_add_fusion.5
  476.9 9.8 %collective-permute-done = bf16[2,256,512]{1,2,0:T(8,128)(2,1)S(1)} collective-permute-done((bf16[2,256,512]{1,2,0:T(8,128)(2,1)S(1)}, bf16[2,256,512]{1,2,0:T(8,128)(2,1)S(1)}, u32[]{:S(2)}, u32[]{:S(2)}) %collective-permute-start) | collective-permute-done | bytes 524320 | tf_op jit(solution)/shard_map/while/body/eval_jaxpr/ppermute | solution.py:11
  497.1 9.8 %collective-permute-done = bf16[2,256,512]{1,2,0:T(8,128)(2,1)S(1)} collective-permute-done((bf16[2,256,512]{1,2,0:T(8,128)(2,1)S(1)}, bf16[2,256,512]{1,2,0:T(8,128)(2,1)S(1)}, u32[]{:S(2)}, u32[]{:S(2)}) %collective-permute-start) | collective-permute-done | bytes 524320 | tf_op jit(solution)/shard_map/while/body/eval_jaxpr/ppermute | solution.py:11
  517.2 9.8 %collective-permute-done = bf16[2,256,512]{1,2,0:T(8,128)(2,1)S(1)} collective-permute-done((bf16[2,256,512]{1,2,0:T(8,128)(2,1)S(1)}, bf16[2,256,512]{1,2,0:T(8,128)(2,1)S(1)}, u32[]{:S(2)}, u32[]{:S(2)}) %collective-permute-start) | collective-permute-done | bytes 524320 | tf_op jit(solution)/shard_map/while/body/eval_jaxpr/ppermute | solution.py:11
  537.4 9.8 %collective-permute-done = bf16[2,256,512]{1,2,0:T(8,128)(2,1)S(1)} collective-permute-done((bf16[2,256,512]{1,2,0:T(8,128)(2,1)S(1)}, bf16[2,256,512]{1,2,0:T(8,128)(2,1)S(1)}, u32[]{:S(2)}, u32[]{:S(2)}) %collective-permute-start) | collective-permute-done | bytes 524320 | tf_op jit(solution)/shard_map/while/body/eval_jaxpr/ppermute | solution.py:11
  557.5 9.8 %collective-permute-done = bf16[2,256,512]{1,2,0:T(8,128)(2,1)S(1)} collective-permute-done((bf16[2,256,512]{1,2,0:T(8,128)(2,1)S(1)}, bf16[2,256,512]{1,2,0:T(8,128)(2,1)S(1)}, u32[]{:S(2)}, u32[]{:S(2)}) %collective-permute-start) | collective-permute-done | bytes 524320 | tf_op jit(solution)/shard_map/while/body/eval_jaxpr/ppermute | solution.py:11
  577.7 9.8 %collective-permute-done = bf16[2,256,512]{1,2,0:T(8,128)(2,1)S(1)} collective-permute-done((bf16[2,256,512]{1,2,0:T(8,128)(2,1)S(1)}, bf16[2,256,512]{1,2,0:T(8,128)(2,1)S(1)}, u32[]{:S(2)}, u32[]{:S(2)}) %collective-permute-start) | collective-permute-done | bytes 524320 | tf_op jit(solution)/shard_map/while/body/eval_jaxpr/ppermute | solution.py:11
  597.8 9.8 %collective-permute-done = bf16[2,256,512]{1,2,0:T(8,128)(2,1)S(1)} collective-permute-done((bf16[2,256,512]{1,2,0:T(8,128)(2,1)S(1)}, bf16[2,256,512]{1,2,0:T(8,128)(2,1)S(1)}, u32[]{:S(2)}, u32[]{:S(2)}) %collective-permute-start) | collective-permute-done | bytes 524320 | tf_op jit(solution)/shard_map/while/body/eval_jaxpr/ppermute | solution.py:11
  618.0 9.8 %collective-permute-done = bf16[2,256,512]{1,2,0:T(8,128)(2,1)S(1)} collective-permute-done((bf16[2,256,512]{1,2,0:T(8,128)(2,1)S(1)}, bf16[2,256,512]{1,2,0:T(8,128)(2,1)S(1)}, u32[]{:S(2)}, u32[]{:S(2)}) %collective-permute-start) | collective-permute-done | bytes 524320 | tf_op jit(solution)/shard_map/while/body/eval_jaxpr/ppermute | solution.py:11
  638.1 9.8 %collective-permute-done = bf16[2,256,512]{1,2,0:T(8,128)(2,1)S(1)} collective-permute-done((bf16[2,256,512]{1,2,0:T(8,128)(2,1)S(1)}, bf16[2,256,512]{1,2,0:T(8,128)(2,1)S(1)}, u32[]{:S(2)}, u32[]{:S(2)}) %collective-permute-start) | collective-permute-done | bytes 524320 | tf_op jit(solution)/shard_map/while/body/eval_jaxpr/ppermute | solution.py:11
  658.3 9.8 %collective-permute-done = bf16[2,256,512]{1,2,0:T(8,128)(2,1)S(1)} collective-permute-done((bf16[2,256,512]{1,2,0:T(8,128)(2,1)S(1)}, bf16[2,256,512]{1,2,0:T(8,128)(2,1)S(1)}, u32[]{:S(2)}, u32[]{:S(2)}) %collective-permute-start) | collective-permute-done | bytes 524320 | tf_op jit(solution)/shard_map/while/body/eval_jaxpr/ppermute | solution.py:11
  678.4 9.8 %collective-permute-done = bf16[2,256,512]{1,2,0:T(8,128)(2,1)S(1)} collective-permute-done((bf16[2,256,512]{1,2,0:T(8,128)(2,1)S(1)}, bf16[2,256,512]{1,2,0:T(8,128)(2,1)S(1)}, u32[]{:S(2)}, u32[]{:S(2)}) %collective-permute-start) | collective-permute-done | bytes 524320 | tf_op jit(solution)/shard_map/while/body/eval_jaxpr/ppermute | solution.py:11
  698.6 9.8 %collective-permute-done = bf16[2,256,512]{1,2,0:T(8,128)(2,1)S(1)} collective-permute-done((bf16[2,256,512]{1,2,0:T(8,128)(2,1)S(1)}, bf16[2,256,512]{1,2,0:T(8,128)(2,1)S(1)}, u32[]{:S(2)}, u32[]{:S(2)}) %collective-permute-start) | collective-permute-done | bytes 524320 | tf_op jit(solution)/shard_map/while/body/eval_jaxpr/ppermute | solution.py:11
  718.7 9.8 %collective-permute-done = bf16[2,256,512]{1,2,0:T(8,128)(2,1)S(1)} collective-permute-done((bf16[2,256,512]{1,2,0:T(8,128)(2,1)S(1)}, bf16[2,256,512]{1,2,0:T(8,128)(2,1)S(1)}, u32[]{:S(2)}, u32[]{:S(2)}) %collective-permute-start) | collective-permute-done | bytes 524320 | tf_op jit(solution)/shard_map/while/body/eval_jaxpr/ppermute | solution.py:11
  (278 shorter events, 164.1 us)
Async XLA Ops:
  6.5 9.3 %copy-start.3 = (s32[1,32]{1,0:T(1,128)S(1)}, s32[1,32]{1,0:T(1,128)}, u32[]{:S(2)}) copy-start(s32[1,32]{1,0:T(1,128)} %param.10) | copy-start | bytes 388
  6.5 208.3 %all-gather.5.cloned.1.call-start = ((), (), s32[]{:S(2)}) async-start(), calls=%async_computation.1 | async-start | bytes 8454144 | tf_op jit(solution)/shard_map/all_gather | solution.py:42
  7.3 411.0 %all-gather.3.cloned.1.call-start = ((), (), s32[]{:S(2)}) async-start(), calls=%async_computation | async-start | bytes 8454144 | tf_op jit(solution)/shard_map/all_gather | solution.py:37
  425.5 5.4 copy-start.2
  435.7 10.7 %collective-permute-start = (bf16[2,256,512]{1,2,0:T(8,128)(2,1)S(1)}, bf16[2,256,512]{1,2,0:T(8,128)(2,1)S(1)}, u32[]{:S(2)}, u32[]{:S(2)}) collective-permute-start(bf16[2,256,512]{1,2,0:T(8,128)(2,1)S(1)} %get-tuple-element.491), channel_id=1, source_target_pairs={{0,1},{1,2},{2,3},{3,4},{4,5},{5,6},{6,7},{7,8},{8,9},{9,10},{10,1... | collective-permute-start | bytes 1572872 | tf_op jit(solution)/shard_map/while/body/eval_jaxpr/ppermute | solution.py:11
  455.9 10.7 %collective-permute-start = (bf16[2,256,512]{1,2,0:T(8,128)(2,1)S(1)}, bf16[2,256,512]{1,2,0:T(8,128)(2,1)S(1)}, u32[]{:S(2)}, u32[]{:S(2)}) collective-permute-start(bf16[2,256,512]{1,2,0:T(8,128)(2,1)S(1)} %get-tuple-element.491), channel_id=1, source_target_pairs={{0,1},{1,2},{2,3},{3,4},{4,5},{5,6},{6,7},{7,8},{8,9},{9,10},{10,1... | collective-permute-start | bytes 1572872 | tf_op jit(solution)/shard_map/while/body/eval_jaxpr/ppermute | solution.py:11
  476.0 10.7 %collective-permute-start = (bf16[2,256,512]{1,2,0:T(8,128)(2,1)S(1)}, bf16[2,256,512]{1,2,0:T(8,128)(2,1)S(1)}, u32[]{:S(2)}, u32[]{:S(2)}) collective-permute-start(bf16[2,256,512]{1,2,0:T(8,128)(2,1)S(1)} %get-tuple-element.491), channel_id=1, source_target_pairs={{0,1},{1,2},{2,3},{3,4},{4,5},{5,6},{6,7},{7,8},{8,9},{9,10},{10,1... | collective-permute-start | bytes 1572872 | tf_op jit(solution)/shard_map/while/body/eval_jaxpr/ppermute | solution.py:11
  486.8 3.7 copy-start
  496.2 10.7 %collective-permute-start = (bf16[2,256,512]{1,2,0:T(8,128)(2,1)S(1)}, bf16[2,256,512]{1,2,0:T(8,128)(2,1)S(1)}, u32[]{:S(2)}, u32[]{:S(2)}) collective-permute-start(bf16[2,256,512]{1,2,0:T(8,128)(2,1)S(1)} %get-tuple-element.491), channel_id=1, source_target_pairs={{0,1},{1,2},{2,3},{3,4},{4,5},{5,6},{6,7},{7,8},{8,9},{9,10},{10,1... | collective-permute-start | bytes 1572872 | tf_op jit(solution)/shard_map/while/body/eval_jaxpr/ppermute | solution.py:11
  516.3 10.7 %collective-permute-start = (bf16[2,256,512]{1,2,0:T(8,128)(2,1)S(1)}, bf16[2,256,512]{1,2,0:T(8,128)(2,1)S(1)}, u32[]{:S(2)}, u32[]{:S(2)}) collective-permute-start(bf16[2,256,512]{1,2,0:T(8,128)(2,1)S(1)} %get-tuple-element.491), channel_id=1, source_target_pairs={{0,1},{1,2},{2,3},{3,4},{4,5},{5,6},{6,7},{7,8},{8,9},{9,10},{10,1... | collective-permute-start | bytes 1572872 | tf_op jit(solution)/shard_map/while/body/eval_jaxpr/ppermute | solution.py:11
  527.1 3.7 copy-start
  536.5 10.7 %collective-permute-start = (bf16[2,256,512]{1,2,0:T(8,128)(2,1)S(1)}, bf16[2,256,512]{1,2,0:T(8,128)(2,1)S(1)}, u32[]{:S(2)}, u32[]{:S(2)}) collective-permute-start(bf16[2,256,512]{1,2,0:T(8,128)(2,1)S(1)} %get-tuple-element.491), channel_id=1, source_target_pairs={{0,1},{1,2},{2,3},{3,4},{4,5},{5,6},{6,7},{7,8},{8,9},{9,10},{10,1... | collective-permute-start | bytes 1572872 | tf_op jit(solution)/shard_map/while/body/eval_jaxpr/ppermute | solution.py:11
  556.6 10.7 %collective-permute-start = (bf16[2,256,512]{1,2,0:T(8,128)(2,1)S(1)}, bf16[2,256,512]{1,2,0:T(8,128)(2,1)S(1)}, u32[]{:S(2)}, u32[]{:S(2)}) collective-permute-start(bf16[2,256,512]{1,2,0:T(8,128)(2,1)S(1)} %get-tuple-element.491), channel_id=1, source_target_pairs={{0,1},{1,2},{2,3},{3,4},{4,5},{5,6},{6,7},{7,8},{8,9},{9,10},{10,1... | collective-permute-start | bytes 1572872 | tf_op jit(solution)/shard_map/while/body/eval_jaxpr/ppermute | solution.py:11
  567.4 3.7 copy-start
  576.8 10.7 %collective-permute-start = (bf16[2,256,512]{1,2,0:T(8,128)(2,1)S(1)}, bf16[2,256,512]{1,2,0:T(8,128)(2,1)S(1)}, u32[]{:S(2)}, u32[]{:S(2)}) collective-permute-start(bf16[2,256,512]{1,2,0:T(8,128)(2,1)S(1)} %get-tuple-element.491), channel_id=1, source_target_pairs={{0,1},{1,2},{2,3},{3,4},{4,5},{5,6},{6,7},{7,8},{8,9},{9,10},{10,1... | collective-permute-start | bytes 1572872 | tf_op jit(solution)/shard_map/while/body/eval_jaxpr/ppermute | solution.py:11
  596.9 10.7 %collective-permute-start = (bf16[2,256,512]{1,2,0:T(8,128)(2,1)S(1)}, bf16[2,256,512]{1,2,0:T(8,128)(2,1)S(1)}, u32[]{:S(2)}, u32[]{:S(2)}) collective-permute-start(bf16[2,256,512]{1,2,0:T(8,128)(2,1)S(1)} %get-tuple-element.491), channel_id=1, source_target_pairs={{0,1},{1,2},{2,3},{3,4},{4,5},{5,6},{6,7},{7,8},{8,9},{9,10},{10,1... | collective-permute-start | bytes 1572872 | tf_op jit(solution)/shard_map/while/body/eval_jaxpr/ppermute | solution.py:11
  607.7 3.7 copy-start
  617.1 10.7 %collective-permute-start = (bf16[2,256,512]{1,2,0:T(8,128)(2,1)S(1)}, bf16[2,256,512]{1,2,0:T(8,128)(2,1)S(1)}, u32[]{:S(2)}, u32[]{:S(2)}) collective-permute-start(bf16[2,256,512]{1,2,0:T(8,128)(2,1)S(1)} %get-tuple-element.491), channel_id=1, source_target_pairs={{0,1},{1,2},{2,3},{3,4},{4,5},{5,6},{6,7},{7,8},{8,9},{9,10},{10,1... | collective-permute-start | bytes 1572872 | tf_op jit(solution)/shard_map/while/body/eval_jaxpr/ppermute | solution.py:11
  637.2 10.7 %collective-permute-start = (bf16[2,256,512]{1,2,0:T(8,128)(2,1)S(1)}, bf16[2,256,512]{1,2,0:T(8,128)(2,1)S(1)}, u32[]{:S(2)}, u32[]{:S(2)}) collective-permute-start(bf16[2,256,512]{1,2,0:T(8,128)(2,1)S(1)} %get-tuple-element.491), channel_id=1, source_target_pairs={{0,1},{1,2},{2,3},{3,4},{4,5},{5,6},{6,7},{7,8},{8,9},{9,10},{10,1... | collective-permute-start | bytes 1572872 | tf_op jit(solution)/shard_map/while/body/eval_jaxpr/ppermute | solution.py:11
  648.0 3.7 copy-start
  657.4 10.7 %collective-permute-start = (bf16[2,256,512]{1,2,0:T(8,128)(2,1)S(1)}, bf16[2,256,512]{1,2,0:T(8,128)(2,1)S(1)}, u32[]{:S(2)}, u32[]{:S(2)}) collective-permute-start(bf16[2,256,512]{1,2,0:T(8,128)(2,1)S(1)} %get-tuple-element.491), channel_id=1, source_target_pairs={{0,1},{1,2},{2,3},{3,4},{4,5},{5,6},{6,7},{7,8},{8,9},{9,10},{10,1... | collective-permute-start | bytes 1572872 | tf_op jit(solution)/shard_map/while/body/eval_jaxpr/ppermute | solution.py:11
  677.5 10.7 %collective-permute-start = (bf16[2,256,512]{1,2,0:T(8,128)(2,1)S(1)}, bf16[2,256,512]{1,2,0:T(8,128)(2,1)S(1)}, u32[]{:S(2)}, u32[]{:S(2)}) collective-permute-start(bf16[2,256,512]{1,2,0:T(8,128)(2,1)S(1)} %get-tuple-element.491), channel_id=1, source_target_pairs={{0,1},{1,2},{2,3},{3,4},{4,5},{5,6},{6,7},{7,8},{8,9},{9,10},{10,1... | collective-permute-start | bytes 1572872 | tf_op jit(solution)/shard_map/while/body/eval_jaxpr/ppermute | solution.py:11
  697.7 10.7 %collective-permute-start = (bf16[2,256,512]{1,2,0:T(8,128)(2,1)S(1)}, bf16[2,256,512]{1,2,0:T(8,128)(2,1)S(1)}, u32[]{:S(2)}, u32[]{:S(2)}) collective-permute-start(bf16[2,256,512]{1,2,0:T(8,128)(2,1)S(1)} %get-tuple-element.491), channel_id=1, source_target_pairs={{0,1},{1,2},{2,3},{3,4},{4,5},{5,6},{6,7},{7,8},{8,9},{9,10},{10,1... | collective-permute-start | bytes 1572872 | tf_op jit(solution)/shard_map/while/body/eval_jaxpr/ppermute | solution.py:11
  717.8 10.7 %collective-permute-start = (bf16[2,256,512]{1,2,0:T(8,128)(2,1)S(1)}, bf16[2,256,512]{1,2,0:T(8,128)(2,1)S(1)}, u32[]{:S(2)}, u32[]{:S(2)}) collective-permute-start(bf16[2,256,512]{1,2,0:T(8,128)(2,1)S(1)} %get-tuple-element.491), channel_id=1, source_target_pairs={{0,1},{1,2},{2,3},{3,4},{4,5},{5,6},{6,7},{7,8},{8,9},{9,10},{10,1... | collective-permute-start | bytes 1572872 | tf_op jit(solution)/shard_map/while/body/eval_jaxpr/ppermute | solution.py:11
  (25 other events, 66.3 us)
Sparse Core Ops, SparseCore 0:
  9.1 205.7 all-gather.4
  216.6 201.5 all-gather.2
where the time goes:
time: 752 us; the launch traced here: 751 us
  waiting for transfers between devices  543 us (72%)
  matrix products  101 us (13%)
  other arithmetic  50.9 us (7%)
  local copies, waits for them, and re-layouts  41.2 us (5%)
  between operations  14.2 us (2%)
    all_gather x1, waiting for transfers between devices, per_device(): lax.all_gather(value_matrix, ('dp', 'ctx'), axis=0, tiled=True)  199 us
    all_gather x1, waiting for transfers between devices, per_device(): lax.all_gather(key_matrix, ('dp', 'ctx'), axis=0, tiled=True)  196 us
    ppermute x15, waiting for transfers between devices, shifted(): lax.ppermute(shard, axis, [(i, (i + by) % size) for i in range(size)])  147 us
    dot_general x16, matrix products, attend(): jnp.einsum('ghqk,kga->ghqa', probs, value_row_set, preferred_element_type...  60.5 us
    reduce_sum x16, other arithmetic, attend(): total = total * factor + jnp.sum(weights, axis=-1)  33.8 us
    while x90, local copies, waits for them, and re-layouts  28.9 us
    dot_general x16, matrix products, attend(): jnp.einsum('qgha,kga->ghqk', query_rows, key_row_set, preferred_element_t...  26.2 us
  transfers between devices with their start and end apart: 17, of which 17 were waited for; matrix products, arithmetic and copies ran while one was open for 4% of the time, Pallas kernels for 0%

commit v1 on v0

--- a/solution.py
+++ b/solution.py
@@ -1,9 +1,26 @@
+import functools
 import jax
 import jax.numpy as jnp
 from jax import lax
 from jax.sharding import PartitionSpec as P
+from jax.lax import all_to_all, axis_size
 
 HEAD_WIDTH = 128
+
+
+def _watch_masks(target, net_axis):
+    return jnp.concatenate(
+        all_to_all(
+            jnp.stack(axis_size(net_axis) * [target]),
+            axis_name=net_axis,
+            split_axis=0,
+            concat_axis=0,
+        ),
+        axis=0,
+    )
+
+
+match_kinds_now = functools.partial(_watch_masks, net_axis=("dp", "ctx"))
 
 
 def shifted(shard, axis, by):
@@ -37,11 +54,7 @@
         lax.all_gather(key_matrix, ("dp", "ctx"), axis=0, tiled=True),
         preferred_element_type=jnp.float32,
     )
-    values_full = jnp.dot(
-        tokens,
-        lax.all_gather(value_matrix, ("dp", "ctx"), axis=0, tiled=True),
-        preferred_element_type=jnp.float32,
-    )
+    values_full = jnp.dot(tokens, match_kinds_now(value_matrix), preferred_element_type=jnp.float32)
     stacked = jnp.stack((keys_full.astype(jnp.bfloat16), values_full.astype(jnp.bfloat16)), axis=0)
     query_rows = queries[0].reshape(rows, kv_heads, group_size, head_size)
     query_pos = positions(here * rows, rows)

time: 752 us -> 635 us (0.84)
  waiting for transfers between devices: 543 us -> 405 us
  starting transfers between devices: 0.08 us -> 11.7 us
    all_gather x1 -> x0, waiting for transfers between devices: 199 us -> none  [per_device(): lax.all_gather(value_matrix, ('dp', 'ctx'), axis=0, tiled=True)]
    all_to_all x0 -> x1, waiting for transfers between devices: none -> 107 us  [_watch_masks(): all_to_all(jnp.stack(axis_size(net_axis) * [target]), axis_name=net_axis,...]
    all_gather x1, waiting for transfers between devices: 196 us -> 151 us  [per_device(): lax.all_gather(key_matrix, ('dp', 'ctx'), axis=0, tiled=True)]
    all_to_all x0 -> x1, starting transfers between devices: none -> 11.7 us  [_watch_masks(): all_to_all(jnp.stack(axis_size(net_axis) * [target]), axis_name=net_axis,...]
  transfers between devices with their start and end apart: 17 -> 17, of which waited for: 17 -> 17; matrix products, arithmetic and copies ran while one was open for 4% -> 5% of each run, Pallas kernels for 0% -> 0%
where the time goes in v1:
time: 635 us
  waiting for transfers between devices  405 us (64%)
  matrix products  103 us (16%)
  other arithmetic  51.7 us (8%)
  local copies, waits for them, and re-layouts  47.5 us (7%)
  between operations  14.2 us (2%)
  starting transfers between devices  11.7 us (2%)
    all_gather x1, waiting for transfers between devices, per_device(): lax.all_gather(key_matrix, ('dp', 'ctx'), axis=0, tiled=True)  151 us
    ppermute x15, waiting for transfers between devices, shifted(): lax.ppermute(shard, axis, [(i, (i + by) % size) for i in range(size)])  147 us
    all_to_all x1, waiting for transfers between devices, _watch_masks(): all_to_all(jnp.stack(axis_size(net_axis) * [target]), axis_name=net_axis,...  107 us
    dot_general x16, matrix products, attend(): jnp.einsum('ghqk,kga->ghqa', probs, value_row_set, preferred_element_type...  63.1 us
    reduce_sum x16, other arithmetic, attend(): total = total * factor + jnp.sum(weights, axis=-1)  34 us
    while x90, local copies, waits for them, and re-layouts  29.2 us
    dot_general x16, matrix products, attend(): jnp.einsum('qgha,kga->ghqk', query_rows, key_row_set, preferred_element_t...  25.7 us
  transfers between devices with their start and end apart: 17, of which 17 were waited for; matrix products, arithmetic and copies ran while one was open for 5% of the time, Pallas kernels for 0%

profile of v1, /device:TPU:0, one launch (start us, length us, event | category | flops | bytes accessed | tf_op | source)
XLA Modules:
  0.0 634.7 jit_solution(11072544672746272154)
XLA Ops:
  7.3 5.1 stack.8
  12.4 11.7 %all-to-all-start = ((bf16[128,64,512]{2,1,0:T(8,128)(2,1)}), bf16[128,64,512]{2,1,0:T(8,128)(2,1)}, u32[]{:S(2)}, u32[]{:S(2)}) async-start(bf16[128,64,512]{2,1,0:T(8,128)(2,1)} %stack.8), calls=%async_computation | async-start | bytes 16777216 | tf_op jit(solution)/shard_map/all_to_all | solution.py:13
  30.5 107.1 %all-to-all-done = bf16[128,64,512]{2,1,0:T(8,128)(2,1)} async-done(((bf16[128,64,512]{2,1,0:T(8,128)(2,1)}), bf16[128,64,512]{2,1,0:T(8,128)(2,1)}, u32[]{:S(2)}, u32[]{:S(2)}) %all-to-all-start) | async-done | bytes 8388640 | tf_op jit(solution)/shard_map/all_to_all | solution.py:13
  137.6 7.0 %fusion.39 = bf16[256,512]{1,0:T(8,128)(2,1)S(1)} fusion(bf16[8192,512]{1,0:T(8,128)(2,1)} %bitcast.6, bf16[1,256,8192]{2,1,0:T(8,128)(2,1)} %param.8), kind=kOutput, calls=%fused_computation.51 | convolution fusion | flops 2147614720 | bytes 12845056 | tf_op jit(solution)/shard_map/dot_general | solution.py:57
  144.7 150.5 %all-gather.2.cloned.1.call-done = bf16[8192,512]{1,0:T(8,128)(2,1)} async-done(((bf16[64,512]{1,0:T(8,128)(2,1)}), bf16[8192,512]{1,0:T(8,128)(2,1)}) %all-gather.2.cloned.1.call-update) | async-done | bytes 8388624 | tf_op jit(solution)/shard_map/all_gather | solution.py:54
  295.2 7.0 %fusion.36 = bf16[256,512]{1,0:T(8,128)(2,1)S(1)} fusion(bf16[8192,512]{1,0:T(8,128)(2,1)} %all-gather.2.cloned.1.call-done, bf16[1,256,8192]{2,1,0:T(8,128)(2,1)} %param.8), kind=kOutput, calls=%fused_computation.50 | convolution fusion | flops 2147614720 | bytes 12845056 | tf_op jit(solution)/shard_map/dot_general | solution.py:52
  311.6 7.0 %broadcast_add_fusion = f32[4,8,256,128]{3,2,1,0:T(8,128)} fusion(f32[4,8,256]{2,1,0:T(8,128)} %get-tuple-element.388, f32[4,256,256,8]{2,1,3,0:T(8,128)} %copy-done, f32[4,8,256]{2,1,0:T(8,128)S(1)} %broadcast_maximum_fusion, pred[256,256]{0,1:T(8,128)(4,1)S(1)} %or_and_fusion.1, bf16[256,4,128,1]{2,1,0,3:T(4,128)(2,1)S(1)} %bitcast.91), kind=kOutput, calls=%fused_computation.48 | convolution fusion | flops 548405248 | bytes 12976128 | tf_op jit(solution)/shard_map/ghqk,kga->ghqa/dot_general | solution.py:83
  318.5 302.8 %while.23 = (s32[]{:T(128)}, f32[4,8,256]{2,1,0:T(8,128)S(1)}, f32[4,8,256]{2,1,0:T(8,128)S(1)}, f32[4,8,256,128]{3,2,1,0:T(8,128)}, bf16[2,256,512]{1,2,0:T(8,1...) while((s32[]{:T(128)}, f32[4,8,256]{2,1,0:T(8,128)S(1)}, ...), condition=%wide.region_7.8_spmd.clone, body=%wide.region_3.7_spmd.clone.sunk | while | flops 1103347456 | bytes 74720784 | solution.py:101
  319.4 9.8 %collective-permute-done = bf16[2,256,512]{1,2,0:T(8,128)(2,1)S(1)} collective-permute-done((bf16[2,256,512]{1,2,0:T(8,128)(2,1)S(1)}, bf16[2,256,512]{1,2,0:T(8,128)(2,1)S(1)}, u32[]{:S(2)}, u32[]{:S(2)}) %collective-permute-start) | collective-permute-done | bytes 524320 | tf_op jit(solution)/shard_map/while/body/eval_jaxpr/ppermute | solution.py:28
  333.0 3.7 multiply_add_fusion.5
  339.6 9.8 %collective-permute-done = bf16[2,256,512]{1,2,0:T(8,128)(2,1)S(1)} collective-permute-done((bf16[2,256,512]{1,2,0:T(8,128)(2,1)S(1)}, bf16[2,256,512]{1,2,0:T(8,128)(2,1)S(1)}, u32[]{:S(2)}, u32[]{:S(2)}) %collective-permute-start) | collective-permute-done | bytes 524320 | tf_op jit(solution)/shard_map/while/body/eval_jaxpr/ppermute | solution.py:28
  359.8 9.8 %collective-permute-done = bf16[2,256,512]{1,2,0:T(8,128)(2,1)S(1)} collective-permute-done((bf16[2,256,512]{1,2,0:T(8,128)(2,1)S(1)}, bf16[2,256,512]{1,2,0:T(8,128)(2,1)S(1)}, u32[]{:S(2)}, u32[]{:S(2)}) %collective-permute-start) | collective-permute-done | bytes 524320 | tf_op jit(solution)/shard_map/while/body/eval_jaxpr/ppermute | solution.py:28
  380.0 9.8 %collective-permute-done = bf16[2,256,512]{1,2,0:T(8,128)(2,1)S(1)} collective-permute-done((bf16[2,256,512]{1,2,0:T(8,128)(2,1)S(1)}, bf16[2,256,512]{1,2,0:T(8,128)(2,1)S(1)}, u32[]{:S(2)}, u32[]{:S(2)}) %collective-permute-start) | collective-permute-done | bytes 524320 | tf_op jit(solution)/shard_map/while/body/eval_jaxpr/ppermute | solution.py:28
  400.2 9.8 %collective-permute-done = bf16[2,256,512]{1,2,0:T(8,128)(2,1)S(1)} collective-permute-done((bf16[2,256,512]{1,2,0:T(8,128)(2,1)S(1)}, bf16[2,256,512]{1,2,0:T(8,128)(2,1)S(1)}, u32[]{:S(2)}, u32[]{:S(2)}) %collective-permute-start) | collective-permute-done | bytes 524320 | tf_op jit(solution)/shard_map/while/body/eval_jaxpr/ppermute | solution.py:28
  420.4 9.8 %collective-permute-done = bf16[2,256,512]{1,2,0:T(8,128)(2,1)S(1)} collective-permute-done((bf16[2,256,512]{1,2,0:T(8,128)(2,1)S(1)}, bf16[2,256,512]{1,2,0:T(8,128)(2,1)S(1)}, u32[]{:S(2)}, u32[]{:S(2)}) %collective-permute-start) | collective-permute-done | bytes 524320 | tf_op jit(solution)/shard_map/while/body/eval_jaxpr/ppermute | solution.py:28
  440.6 9.8 %collective-permute-done = bf16[2,256,512]{1,2,0:T(8,128)(2,1)S(1)} collective-permute-done((bf16[2,256,512]{1,2,0:T(8,128)(2,1)S(1)}, bf16[2,256,512]{1,2,0:T(8,128)(2,1)S(1)}, u32[]{:S(2)}, u32[]{:S(2)}) %collective-permute-start) | collective-permute-done | bytes 524320 | tf_op jit(solution)/shard_map/while/body/eval_jaxpr/ppermute | solution.py:28
  460.7 9.8 %collective-permute-done = bf16[2,256,512]{1,2,0:T(8,128)(2,1)S(1)} collective-permute-done((bf16[2,256,512]{1,2,0:T(8,128)(2,1)S(1)}, bf16[2,256,512]{1,2,0:T(8,128)(2,1)S(1)}, u32[]{:S(2)}, u32[]{:S(2)}) %collective-permute-start) | collective-permute-done | bytes 524320 | tf_op jit(solution)/shard_map/while/body/eval_jaxpr/ppermute | solution.py:28
  480.9 9.8 %collective-permute-done = bf16[2,256,512]{1,2,0:T(8,128)(2,1)S(1)} collective-permute-done((bf16[2,256,512]{1,2,0:T(8,128)(2,1)S(1)}, bf16[2,256,512]{1,2,0:T(8,128)(2,1)S(1)}, u32[]{:S(2)}, u32[]{:S(2)}) %collective-permute-start) | collective-permute-done | bytes 524320 | tf_op jit(solution)/shard_map/while/body/eval_jaxpr/ppermute | solution.py:28
  501.1 9.8 %collective-permute-done = bf16[2,256,512]{1,2,0:T(8,128)(2,1)S(1)} collective-permute-done((bf16[2,256,512]{1,2,0:T(8,128)(2,1)S(1)}, bf16[2,256,512]{1,2,0:T(8,128)(2,1)S(1)}, u32[]{:S(2)}, u32[]{:S(2)}) %collective-permute-start) | collective-permute-done | bytes 524320 | tf_op jit(solution)/shard_map/while/body/eval_jaxpr/ppermute | solution.py:28
  521.3 9.8 %collective-permute-done = bf16[2,256,512]{1,2,0:T(8,128)(2,1)S(1)} collective-permute-done((bf16[2,256,512]{1,2,0:T(8,128)(2,1)S(1)}, bf16[2,256,512]{1,2,0:T(8,128)(2,1)S(1)}, u32[]{:S(2)}, u32[]{:S(2)}) %collective-permute-start) | collective-permute-done | bytes 524320 | tf_op jit(solution)/shard_map/while/body/eval_jaxpr/ppermute | solution.py:28
  541.5 9.8 %collective-permute-done = bf16[2,256,512]{1,2,0:T(8,128)(2,1)S(1)} collective-permute-done((bf16[2,256,512]{1,2,0:T(8,128)(2,1)S(1)}, bf16[2,256,512]{1,2,0:T(8,128)(2,1)S(1)}, u32[]{:S(2)}, u32[]{:S(2)}) %collective-permute-start) | collective-permute-done | bytes 524320 | tf_op jit(solution)/shard_map/while/body/eval_jaxpr/ppermute | solution.py:28
  561.7 9.8 %collective-permute-done = bf16[2,256,512]{1,2,0:T(8,128)(2,1)S(1)} collective-permute-done((bf16[2,256,512]{1,2,0:T(8,128)(2,1)S(1)}, bf16[2,256,512]{1,2,0:T(8,128)(2,1)S(1)}, u32[]{:S(2)}, u32[]{:S(2)}) %collective-permute-start) | collective-permute-done | bytes 524320 | tf_op jit(solution)/shard_map/while/body/eval_jaxpr/ppermute | solution.py:28
  581.9 9.8 %collective-permute-done = bf16[2,256,512]{1,2,0:T(8,128)(2,1)S(1)} collective-permute-done((bf16[2,256,512]{1,2,0:T(8,128)(2,1)S(1)}, bf16[2,256,512]{1,2,0:T(8,128)(2,1)S(1)}, u32[]{:S(2)}, u32[]{:S(2)}) %collective-permute-start) | collective-permute-done | bytes 524320 | tf_op jit(solution)/shard_map/while/body/eval_jaxpr/ppermute | solution.py:28
  602.1 9.8 %collective-permute-done = bf16[2,256,512]{1,2,0:T(8,128)(2,1)S(1)} collective-permute-done((bf16[2,256,512]{1,2,0:T(8,128)(2,1)S(1)}, bf16[2,256,512]{1,2,0:T(8,128)(2,1)S(1)}, u32[]{:S(2)}, u32[]{:S(2)}) %collective-permute-start) | collective-permute-done | bytes 524320 | tf_op jit(solution)/shard_map/while/body/eval_jaxpr/ppermute | solution.py:28
  (280 shorter events, 173.0 us)
Async XLA Ops:
  6.5 288.7 %all-gather.2.cloned.1.call-start = ((), (), s32[]{:S(2)}) async-start(), calls=%async_computation.1 | async-start | bytes 8454144 | tf_op jit(solution)/shard_map/all_gather | solution.py:54
  12.4 12.4 %copy-start.3 = (bf16[1,256,4096]{2,1,0:T(8,128)(2,1)S(1)}, bf16[1,256,4096]{2,1,0:T(8,128)(2,1)}, u32[]{:S(2)}) copy-start(bf16[1,256,4096]{2,1,0:T(8,128)(2,1)} %param.9) | copy-start | bytes 6291460
  12.4 125.2 %all-to-all-start = ((bf16[128,64,512]{2,1,0:T(8,128)(2,1)}), bf16[128,64,512]{2,1,0:T(8,128)(2,1)}, u32[]{:S(2)}, u32[]{:S(2)}) async-start(bf16[128,64,512]{2,1,0:T(8,128)(2,1)} %stack.8), calls=%async_computation | async-start | bytes 16777216 | tf_op jit(solution)/shard_map/all_to_all | solution.py:13
  24.0 6.2 copy-start.4
  318.5 10.7 %collective-permute-start = (bf16[2,256,512]{1,2,0:T(8,128)(2,1)S(1)}, bf16[2,256,512]{1,2,0:T(8,128)(2,1)S(1)}, u32[]{:S(2)}, u32[]{:S(2)}) collective-permute-start(bf16[2,256,512]{1,2,0:T(8,128)(2,1)S(1)} %get-tuple-element.491), channel_id=1, source_target_pairs={{0,1},{1,2},{2,3},{3,4},{4,5},{5,6},{6,7},{7,8},{8,9},{9,10},{10,1... | collective-permute-start | bytes 1572872 | tf_op jit(solution)/shard_map/while/body/eval_jaxpr/ppermute | solution.py:28
  329.3 3.7 copy-start.1
  338.7 10.7 %collective-permute-start = (bf16[2,256,512]{1,2,0:T(8,128)(2,1)S(1)}, bf16[2,256,512]{1,2,0:T(8,128)(2,1)S(1)}, u32[]{:S(2)}, u32[]{:S(2)}) collective-permute-start(bf16[2,256,512]{1,2,0:T(8,128)(2,1)S(1)} %get-tuple-element.491), channel_id=1, source_target_pairs={{0,1},{1,2},{2,3},{3,4},{4,5},{5,6},{6,7},{7,8},{8,9},{9,10},{10,1... | collective-permute-start | bytes 1572872 | tf_op jit(solution)/shard_map/while/body/eval_jaxpr/ppermute | solution.py:28
  358.9 10.7 %collective-permute-start = (bf16[2,256,512]{1,2,0:T(8,128)(2,1)S(1)}, bf16[2,256,512]{1,2,0:T(8,128)(2,1)S(1)}, u32[]{:S(2)}, u32[]{:S(2)}) collective-permute-start(bf16[2,256,512]{1,2,0:T(8,128)(2,1)S(1)} %get-tuple-element.491), channel_id=1, source_target_pairs={{0,1},{1,2},{2,3},{3,4},{4,5},{5,6},{6,7},{7,8},{8,9},{9,10},{10,1... | collective-permute-start | bytes 1572872 | tf_op jit(solution)/shard_map/while/body/eval_jaxpr/ppermute | solution.py:28
  379.1 10.7 %collective-permute-start = (bf16[2,256,512]{1,2,0:T(8,128)(2,1)S(1)}, bf16[2,256,512]{1,2,0:T(8,128)(2,1)S(1)}, u32[]{:S(2)}, u32[]{:S(2)}) collective-permute-start(bf16[2,256,512]{1,2,0:T(8,128)(2,1)S(1)} %get-tuple-element.491), channel_id=1, source_target_pairs={{0,1},{1,2},{2,3},{3,4},{4,5},{5,6},{6,7},{7,8},{8,9},{9,10},{10,1... | collective-permute-start | bytes 1572872 | tf_op jit(solution)/shard_map/while/body/eval_jaxpr/ppermute | solution.py:28
  389.8 3.7 copy-start.1
  399.3 10.7 %collective-permute-start = (bf16[2,256,512]{1,2,0:T(8,128)(2,1)S(1)}, bf16[2,256,512]{1,2,0:T(8,128)(2,1)S(1)}, u32[]{:S(2)}, u32[]{:S(2)}) collective-permute-start(bf16[2,256,512]{1,2,0:T(8,128)(2,1)S(1)} %get-tuple-element.491), channel_id=1, source_target_pairs={{0,1},{1,2},{2,3},{3,4},{4,5},{5,6},{6,7},{7,8},{8,9},{9,10},{10,1... | collective-permute-start | bytes 1572872 | tf_op jit(solution)/shard_map/while/body/eval_jaxpr/ppermute | solution.py:28
  419.5 10.7 %collective-permute-start = (bf16[2,256,512]{1,2,0:T(8,128)(2,1)S(1)}, bf16[2,256,512]{1,2,0:T(8,128)(2,1)S(1)}, u32[]{:S(2)}, u32[]{:S(2)}) collective-permute-start(bf16[2,256,512]{1,2,0:T(8,128)(2,1)S(1)} %get-tuple-element.491), channel_id=1, source_target_pairs={{0,1},{1,2},{2,3},{3,4},{4,5},{5,6},{6,7},{7,8},{8,9},{9,10},{10,1... | collective-permute-start | bytes 1572872 | tf_op jit(solution)/shard_map/while/body/eval_jaxpr/ppermute | solution.py:28
  430.2 3.7 copy-start.1
  439.6 10.7 %collective-permute-start = (bf16[2,256,512]{1,2,0:T(8,128)(2,1)S(1)}, bf16[2,256,512]{1,2,0:T(8,128)(2,1)S(1)}, u32[]{:S(2)}, u32[]{:S(2)}) collective-permute-start(bf16[2,256,512]{1,2,0:T(8,128)(2,1)S(1)} %get-tuple-element.491), channel_id=1, source_target_pairs={{0,1},{1,2},{2,3},{3,4},{4,5},{5,6},{6,7},{7,8},{8,9},{9,10},{10,1... | collective-permute-start | bytes 1572872 | tf_op jit(solution)/shard_map/while/body/eval_jaxpr/ppermute | solution.py:28
  459.8 10.7 %collective-permute-start = (bf16[2,256,512]{1,2,0:T(8,128)(2,1)S(1)}, bf16[2,256,512]{1,2,0:T(8,128)(2,1)S(1)}, u32[]{:S(2)}, u32[]{:S(2)}) collective-permute-start(bf16[2,256,512]{1,2,0:T(8,128)(2,1)S(1)} %get-tuple-element.491), channel_id=1, source_target_pairs={{0,1},{1,2},{2,3},{3,4},{4,5},{5,6},{6,7},{7,8},{8,9},{9,10},{10,1... | collective-permute-start | bytes 1572872 | tf_op jit(solution)/shard_map/while/body/eval_jaxpr/ppermute | solution.py:28
  480.0 10.7 %collective-permute-start = (bf16[2,256,512]{1,2,0:T(8,128)(2,1)S(1)}, bf16[2,256,512]{1,2,0:T(8,128)(2,1)S(1)}, u32[]{:S(2)}, u32[]{:S(2)}) collective-permute-start(bf16[2,256,512]{1,2,0:T(8,128)(2,1)S(1)} %get-tuple-element.491), channel_id=1, source_target_pairs={{0,1},{1,2},{2,3},{3,4},{4,5},{5,6},{6,7},{7,8},{8,9},{9,10},{10,1... | collective-permute-start | bytes 1572872 | tf_op jit(solution)/shard_map/while/body/eval_jaxpr/ppermute | solution.py:28
  490.8 3.7 copy-start.1
  500.2 10.7 %collective-permute-start = (bf16[2,256,512]{1,2,0:T(8,128)(2,1)S(1)}, bf16[2,256,512]{1,2,0:T(8,128)(2,1)S(1)}, u32[]{:S(2)}, u32[]{:S(2)}) collective-permute-start(bf16[2,256,512]{1,2,0:T(8,128)(2,1)S(1)} %get-tuple-element.491), channel_id=1, source_target_pairs={{0,1},{1,2},{2,3},{3,4},{4,5},{5,6},{6,7},{7,8},{8,9},{9,10},{10,1... | collective-permute-start | bytes 1572872 | tf_op jit(solution)/shard_map/while/body/eval_jaxpr/ppermute | solution.py:28
  520.4 10.7 %collective-permute-start = (bf16[2,256,512]{1,2,0:T(8,128)(2,1)S(1)}, bf16[2,256,512]{1,2,0:T(8,128)(2,1)S(1)}, u32[]{:S(2)}, u32[]{:S(2)}) collective-permute-start(bf16[2,256,512]{1,2,0:T(8,128)(2,1)S(1)} %get-tuple-element.491), channel_id=1, source_target_pairs={{0,1},{1,2},{2,3},{3,4},{4,5},{5,6},{6,7},{7,8},{8,9},{9,10},{10,1... | collective-permute-start | bytes 1572872 | tf_op jit(solution)/shard_map/while/body/eval_jaxpr/ppermute | solution.py:28
  540.6 10.7 %collective-permute-start = (bf16[2,256,512]{1,2,0:T(8,128)(2,1)S(1)}, bf16[2,256,512]{1,2,0:T(8,128)(2,1)S(1)}, u32[]{:S(2)}, u32[]{:S(2)}) collective-permute-start(bf16[2,256,512]{1,2,0:T(8,128)(2,1)S(1)} %get-tuple-element.491), channel_id=1, source_target_pairs={{0,1},{1,2},{2,3},{3,4},{4,5},{5,6},{6,7},{7,8},{8,9},{9,10},{10,1... | collective-permute-start | bytes 1572872 | tf_op jit(solution)/shard_map/while/body/eval_jaxpr/ppermute | solution.py:28
  551.3 3.7 copy-start.1
  560.8 10.7 %collective-permute-start = (bf16[2,256,512]{1,2,0:T(8,128)(2,1)S(1)}, bf16[2,256,512]{1,2,0:T(8,128)(2,1)S(1)}, u32[]{:S(2)}, u32[]{:S(2)}) collective-permute-start(bf16[2,256,512]{1,2,0:T(8,128)(2,1)S(1)} %get-tuple-element.491), channel_id=1, source_target_pairs={{0,1},{1,2},{2,3},{3,4},{4,5},{5,6},{6,7},{7,8},{8,9},{9,10},{10,1... | collective-permute-start | bytes 1572872 | tf_op jit(solution)/shard_map/while/body/eval_jaxpr/ppermute | solution.py:28
  581.0 10.7 %collective-permute-start = (bf16[2,256,512]{1,2,0:T(8,128)(2,1)S(1)}, bf16[2,256,512]{1,2,0:T(8,128)(2,1)S(1)}, u32[]{:S(2)}, u32[]{:S(2)}) collective-permute-start(bf16[2,256,512]{1,2,0:T(8,128)(2,1)S(1)} %get-tuple-element.491), channel_id=1, source_target_pairs={{0,1},{1,2},{2,3},{3,4},{4,5},{5,6},{6,7},{7,8},{8,9},{9,10},{10,1... | collective-permute-start | bytes 1572872 | tf_op jit(solution)/shard_map/while/body/eval_jaxpr/ppermute | solution.py:28
  601.1 10.7 %collective-permute-start = (bf16[2,256,512]{1,2,0:T(8,128)(2,1)S(1)}, bf16[2,256,512]{1,2,0:T(8,128)(2,1)S(1)}, u32[]{:S(2)}, u32[]{:S(2)}) collective-permute-start(bf16[2,256,512]{1,2,0:T(8,128)(2,1)S(1)} %get-tuple-element.491), channel_id=1, source_target_pairs={{0,1},{1,2},{2,3},{3,4},{4,5},{5,6},{6,7},{7,8},{8,9},{9,10},{10,1... | collective-permute-start | bytes 1572872 | tf_op jit(solution)/shard_map/while/body/eval_jaxpr/ppermute | solution.py:28
  (26 other events, 69.7 us)
Sparse Core Ops, SparseCore 0:
  9.1 286.0 all-gather.1
